TPU v7x, 256 devices: a whole 4x4x8 slice. The times are simulated.
256 devices in a mesh: dp: 32 (over x, z), ctx: 8 (over y, core).
Axes of the slice: x: 4, y: 4, z: 8, core: 2. Of those that a mesh axis runs over, the one named last changes fastest.
Arguments:
- hidden: bfloat16 [32, 2048, 4096], P('dp', 'ctx'), may hold values from -6 to 6
- segments: int32 [32, 2048], P('dp', 'ctx'), may hold values from 0 to 15, as said below
- gain: float32 [4096], replicated, may hold values from 0.25 to 1.75
- inv_temp: float32 [], replicated, may hold values from 20 to 50
- positives: int32 [512], P(('dp', 'ctx')), may hold values from 0 to 511, as said below
Outputs:
- grad_hidden: bfloat16 [32, 2048, 4096], P('dp', 'ctx')
- grad_gain: float32 [4096], replicated
- loss: float32 [], replicated
Inputs may be any that keep to these rules, and one draw needn't show every extreme that they name: `segments`: in each sequence the document numbers never fall along positions and every document has one position or more; document 0 covers more than half of the sequence's positions. `positives`: no document is its own positive.
All inputs are finite; a program needn't handle non-finite values.
Results may differ from a plain program's by a relative error of at most 0.0053.
Values may be sent and summed in bfloat16 or wider, within the bound.
A program may use at most 64 MiB of HBM per device.

v0:
```python
import jax
import jax.numpy as jnp
from jax import lax
from jax.sharding import PartitionSpec as P

DOCS_DEV = 2


def normalize_docs(pooled_totals, counts):
    pooled = pooled_totals / counts[:, None]
    rnorm = lax.rsqrt(jnp.sum(pooled * pooled, axis=-1, keepdims=True) + 1e-06)
    return (pooled * rnorm, rnorm)


def body(hidden, segments, gain, inv_temp, positives):
    states = hidden[0].astype(jnp.float32)
    scale_t = lax.rsqrt(jnp.mean(states * states, axis=-1, keepdims=True) + 1e-06)
    normalized_rows = states * scale_t * gain
    ctx_count = lax.axis_size("ctx")
    seq_docs = DOCS_DEV * ctx_count
    document_indicator = (
        segments[0][:, None] == jnp.arange(seq_docs, dtype=jnp.int32)[None, :]
    ).astype(jnp.float32)
    pooled_totals = lax.dot_general(
        document_indicator,
        normalized_rows,
        (((0,), (0,)), ((), ())),
        precision=lax.Precision.HIGHEST,
    )
    counts = jnp.sum(document_indicator, axis=0)
    ctx_rank = lax.axis_index("ctx")
    own_sums, own_counts = (
        lax.psum_scatter(pooled_totals, "ctx", scatter_dimension=0, tiled=True),
        lax.psum_scatter(counts, "ctx", scatter_dimension=0, tiled=True),
    )
    emb_f, rnorm = normalize_docs(own_sums, own_counts)
    emb_own = emb_f.astype(jnp.bfloat16)
    emb_all = lax.all_gather(emb_own, ("dp", "ctx"), axis=0, tiled=True)
    all_docs = emb_all.shape[0]
    row_first = (lax.axis_index("dp") * ctx_count + ctx_rank) * DOCS_DEV
    logits = (
        lax.dot_general(
            emb_own, emb_all, (((1,), (1,)), ((), ())), preferred_element_type=jnp.float32
        )
        * inv_temp
    )
    columns = jnp.arange(all_docs, dtype=jnp.int32)[None, :]
    own_rows = row_first + jnp.arange(DOCS_DEV, dtype=jnp.int32)[:, None]
    pos_mask = (columns == positives[:, None]).astype(jnp.float32)
    logits = jnp.where(columns == own_rows, -1e30, logits)
    top = jnp.max(logits, axis=1, keepdims=True)
    expo = jnp.exp(logits - top)
    total = jnp.sum(expo, axis=1, keepdims=True)
    lse = top[:, 0] + jnp.log(total[:, 0])
    loss_local = jnp.sum(lse - jnp.sum(pos_mask * logits, axis=1)) / all_docs
    gmat = ((expo / total - pos_mask) * (inv_temp / all_docs)).astype(jnp.bfloat16)
    row_grad = jnp.dot(gmat, emb_all, preferred_element_type=jnp.float32)
    grad_rows = lax.all_gather(gmat, ("dp", "ctx"), axis=0, tiled=True)
    grad_cols = lax.dynamic_slice_in_dim(grad_rows, row_first, DOCS_DEV, 1)
    col_grad = lax.dot_general(
        grad_cols, emb_all, (((0,), (0,)), ((), ())), preferred_element_type=jnp.float32
    )
    demb = row_grad + col_grad
    dpool = rnorm * (demb - emb_f * jnp.sum(emb_f * demb, axis=-1, keepdims=True))
    dsum_own = dpool / own_counts[:, None]
    dsum_seq = lax.all_gather(dsum_own, "ctx", axis=0, tiled=True)
    normalized_gradient = jnp.dot(document_indicator, dsum_seq, precision=lax.Precision.HIGHEST)
    gain_local = jnp.sum(normalized_gradient * states * scale_t, axis=0)
    grad_gain, loss = lax.psum((gain_local, loss_local), ("dp", "ctx"))
    grad_out = normalized_gradient * gain
    inner = jnp.mean(grad_out * states, axis=-1, keepdims=True)
    grad_hidden = (scale_t * grad_out - states * scale_t**3 * inner).astype(jnp.bfloat16)
    return (grad_hidden[None], grad_gain, loss)


def solution(mesh):
    return jax.shard_map(
        body,
        mesh=mesh,
        in_specs=(P("dp", "ctx", None), P("dp", "ctx"), P(), P(), P(("dp", "ctx"))),
        out_specs=(P("dp", "ctx", None), P(), P()),
        check_vma=False,
    )
```

profile of v0, /device:TPU:1, one launch (start us, length us, event | category | flops | bytes accessed | tf_op | source)
XLA Modules:
  0.0 389.6 jit_solution(4266364074889755771)
XLA Ops:
  7.2 0.0 copy-start.5
  7.2 0.0 copy-start.4
  7.2 0.0 all-reduce.5.cloned.1.call-start
  7.2 2.1 fusion
  9.3 4.2 %fusion.2 = f32[16,4096]{1,0:T(8,128)} fusion(bf16[1,256,4096]{2,1,0:T(8,128)(2,1)} %param.5, f32[4096]{0:T(1024)} %param.7, f32[256]{0:T(256)S(1)} %get-tuple-element.12, s32[256]{0:T(256)} %bitcast.26), kind=kOutput, calls=%fused_computation.8 | convolution fusion | flops 204476416 | bytes 2377728 | tf_op jit(solution)/shard_map/dot_general | solution.py:24
  13.5 0.0 all-reduce.5.cloned.1.call-update
  13.5 0.0 all-gather.5.cloned.1.call-start
  13.6 0.0 copy-done.5
  13.6 0.6 dynamic-slice
  14.8 0.0 copy-done.4
  14.8 0.1 convert_reduce_fusion
  15.0 15.0 %all-reduce.1 = f32[16]{0:T(128)S(1)} all-reduce(f32[16]{0:T(128)S(1)} %convert_reduce_fusion), channel_id=3, replica_groups=mesh['dp'=32,'ctx'=8] {'ctx'}, use_global_device_ids=true, to_apply=%region_3.0.clone | all-reduce | flops 16 | bytes 128
  29.9 0.1 dynamic-slice.3
  30.0 50.8 %all-reduce.5.cloned.1.call-done = f32[16,4096]{1,0:T(8,128)} async-done(((f32[16,4096]{1,0:T(8,128)}), f32[16,4096]{1,0:T(8,128)}) %all-reduce.5.cloned.1.call-update) | async-done | bytes 262160
  80.8 1.1 multiply_reduce_fusion.1
  81.9 0.7 fusion.30
  82.6 0.0 all-gather.5.cloned.1.call-update
  83.3 119.1 %all-gather.5.cloned.1.call-done = bf16[256,2,4096]{2,1,0:T(2,128)(2,1)} async-done(((bf16[1,2,4096]{2,1,0:T(2,128)(2,1)}), bf16[256,2,4096]{2,1,0:T(2,128)(2,1)}) %all-gather.5.cloned.1.call-update) | async-done | bytes 4194320 | tf_op jit(solution)/shard_map/all_gather | solution.py:38
  202.4 7.2 %reshape.46 = bf16[512,4096]{1,0:T(8,128)(2,1)} reshape(bf16[256,2,4096]{2,1,0:T(2,128)(2,1)} %all-gather.5.cloned.1.call-done) | data formatting | bytes 8388608
  209.6 0.0 copy-start.3
  209.6 0.0 copy-start
  209.6 3.6 fusion.21
  213.3 0.0 copy-done.3
  213.3 0.2 select_reduce_fusion
  213.5 0.1 fusion.29
  213.6 0.0 copy-done
  213.6 0.7 fusion.22
  214.3 0.0 copy-start.1
  214.3 0.0 copy-start.2
  214.3 0.6 subtract_reduce_fusion
  215.6 67.0 %all-gather.1 = bf16[256,2,512]{2,1,0:T(2,128)(2,1)S(1)} all-gather(bf16[1,2,512]{2,1,0:T(2,128)(2,1)S(1)} %fusion.29), channel_id=1, replica_groups=mesh['dp'=32,'ctx'=8] {'dp','ctx'}, dimensions={0}, use_global_device_ids=true | all-gather | bytes 526336 | tf_op jit(solution)/shard_map/all_gather | solution.py:58
  282.6 0.2 reshape.48
  282.8 3.1 multiply_reduce_fusion
  285.9 0.1 divide_bitcast_fusion
  286.0 12.8 %all-gather.2 = f32[8,2,4096]{2,1,0:T(2,128)S(1)} all-gather(f32[1,2,4096]{2,1,0:T(2,128)S(1)} %divide_bitcast_fusion), channel_id=1, replica_groups=mesh['dp'=32,'ctx'=8] {'ctx'}, dimensions={0}, use_global_device_ids=true | all-gather | bytes 294912 | tf_op jit(solution)/shard_map/all_gather | solution.py:66
  298.8 0.2 reshape.50
  299.0 0.0 copy-done.1
  299.0 0.0 copy-done.2
  299.0 4.8 %fusion.9 = (f32[4096]{0:T(1024)S(1)}, f32[256]{0:T(256)S(1)}, f32[256,4096]{1,0:T(8,128)}) fusion(bf16[1,256,4096]{2,1,0:T(8,128)(2,1)S(1)} %copy-done.1, f32[256]{0:T(256)S(1)} %get-tuple-element.12, f32[4096]{0:T(1024)S(1)} %copy-done.2, f32[16,4096]{1,0:T(8,128)S(1)} %reshape.50, s32[256]{0:T(256)S(1)} %bitcast.28), kind=kOutput, calls=%fused_computation.14 | convolution fusion | flops 208666368 | bytes 6589440 | tf_op jit(solution)/shard_map/dot_general | solution.py:67
  303.8 74.0 %all-reduce.2 = (f32[4096]{0:T(1024)}, f32[]{:T(128)}) all-reduce(f32[4096]{0:T(1024)S(1)} %get-tuple-element.3, f32[]{:T(128)S(6)} %div.42), channel_id=1, replica_groups=mesh['dp'=32,'ctx'=8] {'dp','ctx'}, use_global_device_ids=true, to_apply=%region_10.11 | all-reduce | flops 4097 | bytes 32776 | tf_op jit(solution)/shard_map/psum | solution.py:69
  377.8 5.0 %fusion.10 = bf16[1,256,4096]{2,1,0:T(8,128)(2,1)} fusion(f32[256,4096]{1,0:T(8,128)} %get-tuple-element.17, bf16[1,256,4096]{2,1,0:T(8,128)(2,1)S(1)} %copy-done.1, f32[256]{0:T(256)S(1)} %broadcast_multiply_fusion, f32[256]{0:T(256)S(1)} %get-tuple-element.11, f32[4096]{0:T(1024)S(1)} %copy-done.2, f32[256]{0:T(256)S(1)} %get-tuple-element.12), kind=kLoop, calls=%fused_computation.15 | loop fusion | flops 7340032 | bytes 8408064 | tf_op jit(solution)/shard_map/broadcast_in_dim | solution.py:73
  (4 shorter events, 0.0 us)
Async XLA Ops:
  7.2 6.4 %copy-start.5 = (u32[256]{0:T(256)S(1)}, u32[256]{0:T(256)}, u32[]{:S(2)}) copy-start(u32[256]{0:T(256)} %constant.40) | copy-start | bytes 3076
  7.2 7.7 %copy-start.4 = (s32[1,256]{1,0:T(1,128)S(1)}, s32[1,256]{1,0:T(1,128)}, u32[]{:S(2)}) copy-start(s32[1,256]{1,0:T(1,128)} %param.6) | copy-start | bytes 3076
  7.2 73.6 %all-reduce.5.cloned.1.call-start = ((), (), s32[]{:S(2)}) async-start(), calls=%async_computation.1 | async-start | bytes 524288
  13.5 188.9 %all-gather.5.cloned.1.call-start = ((), (), s32[]{:S(2)}) async-start(), calls=%async_computation | async-start | bytes 4210688 | tf_op jit(solution)/shard_map/all_gather | solution.py:38
  209.6 3.6 copy-start.3
  209.6 4.0 %copy-start = (bf16[512,4096]{1,0:T(8,128)(2,1)S(1)}, bf16[512,4096]{1,0:T(8,128)(2,1)}, u32[]{:S(2)}) copy-start(bf16[512,4096]{1,0:T(8,128)(2,1)} %reshape.46) | copy-start | bytes 12582916
  214.3 84.7 %copy-start.1 = (bf16[1,256,4096]{2,1,0:T(8,128)(2,1)S(1)}, bf16[1,256,4096]{2,1,0:T(8,128)(2,1)}, u32[]{:S(2)}) copy-start(bf16[1,256,4096]{2,1,0:T(8,128)(2,1)} %param.5) | copy-start | bytes 6291460
  214.3 84.7 %copy-start.2 = (f32[4096]{0:T(1024)S(1)}, f32[4096]{0:T(1024)}, u32[]{:S(2)}) copy-start(f32[4096]{0:T(1024)} %param.7) | copy-start | bytes 49156
Sparse Core Ops, SparseCore 0:
  13.7 67.1 all-reduce.4
  85.1 117.3 all-gather.4
where the time goes:
time: 390 us
  waiting for transfers between devices  170 us (44%)
  blocking collectives  169 us (43%)
  matrix products  16.3 us (4%)
  between operations  16.1 us (4%)
  other arithmetic  10 us (3%)
  local copies, waits for them, and re-layouts  8.27 us (2%)
    all_gather x1, waiting for transfers between devices, body(): emb_all = lax.all_gather(emb_own, ('dp', 'ctx'), axis=0, tiled=True)  119 us
    psum x1, blocking collectives, body(): grad_gain, loss = lax.psum((gain_local, loss_local), ('dp', 'ctx'))  74 us
    all_gather x1, blocking collectives, body(): grad_rows = lax.all_gather(gmat, ('dp', 'ctx'), axis=0, tiled=True)  67 us
    unnamed x3, waiting for transfers between devices  50.8 us
    unnamed x1, blocking collectives  15 us
    all_gather x1, blocking collectives, body(): dsum_seq = lax.all_gather(dsum_own, 'ctx', axis=0, tiled=True)  12.8 us
    unnamed x17, local copies, waits for them, and re-layouts  8.27 us
  transfers between devices with their start and end apart: 2, of which 2 were waited for; matrix products, arithmetic and copies ran while one was open for 0% of the time, Pallas kernels for 0%

commit v1 on v0

--- a/solution.py
+++ b/solution.py
@@ -66,7 +66,13 @@
     dsum_seq = lax.all_gather(dsum_own, "ctx", axis=0, tiled=True)
     normalized_gradient = jnp.dot(document_indicator, dsum_seq, precision=lax.Precision.HIGHEST)
     gain_local = jnp.sum(normalized_gradient * states * scale_t, axis=0)
-    grad_gain, loss = lax.psum((gain_local, loss_local), ("dp", "ctx"))
+
+    def _launch_table(raw):
+        for idx in ("dp", "ctx"):
+            raw = lax.psum(raw, axis_name=idx)
+        return raw
+
+    grad_gain, loss = _launch_table((gain_local, loss_local))
     grad_out = normalized_gradient * gain
     inner = jnp.mean(grad_out * states, axis=-1, keepdims=True)
     grad_hidden = (scale_t * grad_out - states * scale_t**3 * inner).astype(jnp.bfloat16)

time: 390 us -> 478 us (1.23)
  blocking collectives: 169 us -> 256 us
    psum x1 -> x2, blocking collectives: 74 us -> 162 us  [_launch_table(): raw = lax.psum(raw, axis_name=idx)]
where the time goes in v1:
time: 478 us; the launch traced here: 477 us
  blocking collectives  256 us (54%)
  waiting for transfers between devices  170 us (36%)
  matrix products  16.3 us (3%)
  between operations  16.1 us (3%)
  other arithmetic  10 us (2%)
  local copies, waits for them, and re-layouts  8.27 us (2%)
    psum x2, blocking collectives, _launch_table(): raw = lax.psum(raw, axis_name=idx)  162 us
    all_gather x1, waiting for transfers between devices, body(): emb_all = lax.all_gather(emb_own, ('dp', 'ctx'), axis=0, tiled=True)  119 us
    all_gather x1, blocking collectives, body(): grad_rows = lax.all_gather(gmat, ('dp', 'ctx'), axis=0, tiled=True)  67 us
    unnamed x3, waiting for transfers between devices  50.8 us
    unnamed x1, blocking collectives  15 us
    all_gather x1, blocking collectives, body(): dsum_seq = lax.all_gather(dsum_own, 'ctx', axis=0, tiled=True)  12.8 us
  transfers between devices with their start and end apart: 2, of which 2 were waited for; matrix products, arithmetic and copies ran while one was open for 0% of the time, Pallas kernels for 0%

profile of v1, /device:TPU:1, one launch (start us, length us, event | category | flops | bytes accessed | tf_op | source)
XLA Modules:
  0.0 477.2 jit_solution(16398157103624464069)
XLA Ops:
  7.2 0.0 copy-start.5
  7.2 0.0 copy-start.4
  7.2 0.0 all-reduce.6.cloned.1.call-start
  7.2 2.1 fusion
  9.3 4.2 fusion.2
  13.5 0.0 all-reduce.6.cloned.1.call-update
  13.5 0.0 all-gather.5.cloned.1.call-start
  13.6 0.0 copy-done.5
  13.6 0.6 dynamic-slice
  14.8 0.0 copy-done.4
  14.8 0.1 convert_reduce_fusion
  15.0 15.0 %all-reduce.1 = f32[16]{0:T(128)S(1)} all-reduce(f32[16]{0:T(128)S(1)} %convert_reduce_fusion), channel_id=3, replica_groups=mesh['dp'=32,'ctx'=8] {'ctx'}, use_global_device_ids=true, to_apply=%region_3.0.clone | all-reduce | flops 16 | bytes 128
  29.9 0.1 dynamic-slice.3
  30.0 50.8 %all-reduce.6.cloned.1.call-done = f32[16,4096]{1,0:T(8,128)} async-done(((f32[16,4096]{1,0:T(8,128)}), f32[16,4096]{1,0:T(8,128)}) %all-reduce.6.cloned.1.call-update) | async-done | bytes 262160
  80.8 1.1 multiply_reduce_fusion.1
  81.9 0.7 fusion.30
  82.6 0.0 all-gather.5.cloned.1.call-update
  83.3 119.1 %all-gather.5.cloned.1.call-done = bf16[256,2,4096]{2,1,0:T(2,128)(2,1)} async-done(((bf16[1,2,4096]{2,1,0:T(2,128)(2,1)}), bf16[256,2,4096]{2,1,0:T(2,128)(2,1)}) %all-gather.5.cloned.1.call-update) | async-done | bytes 4194320 | tf_op jit(solution)/shard_map/all_gather | solution.py:38
  202.4 7.2 %reshape.46 = bf16[512,4096]{1,0:T(8,128)(2,1)} reshape(bf16[256,2,4096]{2,1,0:T(2,128)(2,1)} %all-gather.5.cloned.1.call-done) | data formatting | bytes 8388608
  209.6 0.0 copy-start.3
  209.6 0.0 copy-start
  209.6 3.6 fusion.21
  213.3 0.0 copy-done.3
  213.3 0.2 select_reduce_fusion
  213.5 0.1 fusion.29
  213.6 0.0 copy-done
  213.6 0.7 fusion.22
  214.3 0.0 copy-start.1
  214.3 0.0 copy-start.2
  214.3 0.6 subtract_reduce_fusion
  215.6 67.0 %all-gather.1 = bf16[256,2,512]{2,1,0:T(2,128)(2,1)S(1)} all-gather(bf16[1,2,512]{2,1,0:T(2,128)(2,1)S(1)} %fusion.29), channel_id=1, replica_groups=mesh['dp'=32,'ctx'=8] {'dp','ctx'}, dimensions={0}, use_global_device_ids=true | all-gather | bytes 526336 | tf_op jit(solution)/shard_map/all_gather | solution.py:58
  282.6 0.2 reshape.48
  282.8 3.1 multiply_reduce_fusion
  285.9 0.1 divide_bitcast_fusion
  286.0 12.8 %all-gather.2 = f32[8,2,4096]{2,1,0:T(2,128)S(1)} all-gather(f32[1,2,4096]{2,1,0:T(2,128)S(1)} %divide_bitcast_fusion), channel_id=1, replica_groups=mesh['dp'=32,'ctx'=8] {'ctx'}, dimensions={0}, use_global_device_ids=true | all-gather | bytes 294912 | tf_op jit(solution)/shard_map/all_gather | solution.py:66
  298.8 0.2 reshape.50
  299.0 0.0 copy-done.1
  299.0 0.0 copy-done.2
  299.0 4.8 fusion.9
  303.8 112.9 %all-reduce.2 = (f32[4096]{0:T(1024)S(1)}, f32[]{:T(128)}) all-reduce(f32[4096]{0:T(1024)S(1)} %get-tuple-element.3, f32[]{:T(128)S(6)} %div.42), channel_id=1, replica_groups=mesh['dp'=32,'ctx'=8] {'dp'}, use_global_device_ids=true, to_apply=%region_10.11 | all-reduce | flops 4097 | bytes 32776 | tf_op jit(solution)/shard_map/psum | solution.py:72
  416.6 48.7 %all-reduce.3 = (f32[4096]{0:T(1024)}, f32[]{:T(128)}) all-reduce(f32[4096]{0:T(1024)S(1)} %get-tuple-element.7, f32[]{:T(128)} %get-tuple-element.8), channel_id=1, replica_groups=mesh['dp'=32,'ctx'=8] {'ctx'}, use_global_device_ids=true, to_apply=%region_11.12 | all-reduce | flops 4097 | bytes 32776 | tf_op jit(solution)/shard_map/psum | solution.py:72
  465.4 5.0 %fusion.10 = bf16[1,256,4096]{2,1,0:T(8,128)(2,1)} fusion(f32[256,4096]{1,0:T(8,128)} %get-tuple-element.19, bf16[1,256,4096]{2,1,0:T(8,128)(2,1)S(1)} %copy-done.1, f32[256]{0:T(256)S(1)} %broadcast_multiply_fusion, f32[256]{0:T(256)S(1)} %get-tuple-element.13, f32[4096]{0:T(1024)S(1)} %copy-done.2, f32[256]{0:T(256)S(1)} %get-tuple-element.14), kind=kLoop, calls=%fused_computation.15 | loop fusion | flops 7340032 | bytes 8408064 | tf_op jit(solution)/shard_map/broadcast_in_dim | solution.py:79
  (4 shorter events, 0.0 us)
Async XLA Ops:
  7.2 6.4 %copy-start.5 = (u32[256]{0:T(256)S(1)}, u32[256]{0:T(256)}, u32[]{:S(2)}) copy-start(u32[256]{0:T(256)} %constant.40) | copy-start | bytes 3076
  7.2 7.7 %copy-start.4 = (s32[1,256]{1,0:T(1,128)S(1)}, s32[1,256]{1,0:T(1,128)}, u32[]{:S(2)}) copy-start(s32[1,256]{1,0:T(1,128)} %param.6) | copy-start | bytes 3076
  7.2 73.6 %all-reduce.6.cloned.1.call-start = ((), (), s32[]{:S(2)}) async-start(), calls=%async_computation.1 | async-start | bytes 524288
  13.5 188.9 %all-gather.5.cloned.1.call-start = ((), (), s32[]{:S(2)}) async-start(), calls=%async_computation | async-start | bytes 4210688 | tf_op jit(solution)/shard_map/all_gather | solution.py:38
  209.6 3.6 copy-start.3
  209.6 4.0 copy-start
  214.3 84.7 %copy-start.1 = (bf16[1,256,4096]{2,1,0:T(8,128)(2,1)S(1)}, bf16[1,256,4096]{2,1,0:T(8,128)(2,1)}, u32[]{:S(2)}) copy-start(bf16[1,256,4096]{2,1,0:T(8,128)(2,1)} %param.5) | copy-start | bytes 6291460
  214.3 84.7 %copy-start.2 = (f32[4096]{0:T(1024)S(1)}, f32[4096]{0:T(1024)}, u32[]{:S(2)}) copy-start(f32[4096]{0:T(1024)} %param.7) | copy-start | bytes 49156
Sparse Core Ops, SparseCore 0:
  13.7 67.1 all-reduce.5
  85.1 117.3 all-gather.4
